TPU v7x, 256 devices: a whole 4x4x8 slice. The times are simulated.
256 devices in a mesh: nodes: 64 (over x, z, core), mp: 4 (over y).
Axes of the slice: x: 4, y: 4, z: 8, core: 2. Of those that a mesh axis runs over, the one named last changes fastest.
Arguments:
- tokens: bfloat16 [2048, 64, 768], P('nodes'), may hold values from -32 to 32
- w_query: bfloat16 [768, 768], P('mp'), may hold values from -0.5 to 0.5
- w_key: bfloat16 [768, 768], P('mp'), may hold values from -0.5 to 0.5
- w_value: bfloat16 [768, 768], P('mp'), may hold values from -0.21875 to 0.21875
- grad_out: bfloat16 [2048, 12, 4096], P('nodes', 'mp'), may hold values from -6 to 6
- owned_cls: bfloat16 [768, 131072], P('mp', 'nodes'), may hold values from -24 to 24
- send_rows: int32 [64, 64, 32], P('nodes'), may hold values from 0 to 2047
- neigh_slot: int32 [2048, 2, 32], P('nodes'), may hold values from 0 to 2047
- neigh_count: int32 [2048, 2], P('nodes'), may hold values from 1 to 32
Outputs:
- context: bfloat16 [2048, 12, 4096], P('nodes', 'mp')
- grad_query: float32 [768, 768], P('mp')
- grad_key: float32 [768, 768], P('mp')
- grad_value: float32 [768, 768], P('mp')
- grad_cls: float32 [768, 131072], P('mp', 'nodes')
Inputs may be any that keep to these rules, and one draw needn't show every extreme that they name: send_rows[o, r, :] are rows of owner o's own block; rows may repeat. `neigh_slot`: entries with k >= neigh_count[c, t] are not used.
All inputs are finite; a program needn't handle non-finite values.
Results may differ from a plain program's by a relative error of at most 0.012.
The roundings to bfloat16 on the way count: a program that leaves them out, or rounds other values in their place, can miss the bound.
Values may be sent and summed in bfloat16 or wider, within the bound.
No kernel may reach another device: no remote copies, remote signals or barrier semaphores. Data moves between devices by JAX's collectives and lax.ppermute only.
A program may use at most 128 MiB of HBM per device.

v0:
```python
import math
import jax
import jax.numpy as jnp
from jax import lax
from jax.sharding import PartitionSpec as P

HD = 64


def widen_columns(features):
    return lax.all_gather(features, "mp", axis=0, tiled=True)


def local_attend(tokens, virtual, w_query, w_key, w_value, grad_out):
    centres, length, model_width = tokens.shape
    local_width = w_query.shape[0]
    head_count = local_width // HD
    type_count = virtual.shape[1]
    span = type_count + length
    key_input = jnp.concatenate([virtual, tokens], axis=1)
    flat_tokens = tokens.reshape(-1, model_width)
    flat_keys = key_input.reshape(-1, model_width)
    queries = (
        jnp.einsum("nd,od->no", flat_tokens, w_query, preferred_element_type=jnp.float32)
        .astype(jnp.bfloat16)
        .reshape(centres, length, head_count, HD)
    )
    keys = (
        jnp.einsum("nd,od->no", flat_keys, w_key, preferred_element_type=jnp.float32)
        .astype(jnp.bfloat16)
        .reshape(centres, span, head_count, HD)
    )
    values = (
        jnp.einsum("nd,od->no", flat_keys, w_value, preferred_element_type=jnp.float32)
        .astype(jnp.bfloat16)
        .reshape(centres, span, head_count, HD)
    )
    score_scale = 1.0 / math.sqrt(HD)
    scores = (
        jnp.einsum("clhe,cmhe->chlm", queries, keys, preferred_element_type=jnp.float32)
        * score_scale
    )
    attn_probs = jax.nn.softmax(scores, axis=-1)
    probs_low = attn_probs.astype(jnp.bfloat16)
    context = jnp.einsum(
        "chlm,cmhe->chle", probs_low, values, preferred_element_type=jnp.float32
    ).astype(jnp.bfloat16)
    grad_heads = grad_out.reshape(centres, head_count, length, HD)
    prob_grads = jnp.einsum(
        "chle,cmhe->chlm", grad_heads, values, preferred_element_type=jnp.float32
    )
    value_grads = jnp.einsum(
        "chlm,chle->cmhe", probs_low, grad_heads, preferred_element_type=jnp.float32
    ).astype(jnp.bfloat16)
    score_grads = (
        attn_probs
        * (prob_grads - jnp.sum(prob_grads * attn_probs, axis=-1, keepdims=True))
        * score_scale
    )
    score_low = score_grads.astype(jnp.bfloat16)
    query_grads = jnp.einsum(
        "chlm,cmhe->clhe", score_low, keys, preferred_element_type=jnp.float32
    ).astype(jnp.bfloat16)
    key_grads = jnp.einsum(
        "chlm,clhe->cmhe", score_low, queries, preferred_element_type=jnp.float32
    ).astype(jnp.bfloat16)
    part_query = jnp.einsum(
        "no,nd->od",
        query_grads.reshape(-1, local_width),
        flat_tokens,
        preferred_element_type=jnp.float32,
    )
    part_key = jnp.einsum(
        "no,nd->od",
        key_grads.reshape(-1, local_width),
        flat_keys,
        preferred_element_type=jnp.float32,
    )
    part_value = jnp.einsum(
        "no,nd->od",
        value_grads.reshape(-1, local_width),
        flat_keys,
        preferred_element_type=jnp.float32,
    )
    virtual_key = key_grads[:, :type_count].reshape(-1, local_width)
    virtual_value = value_grads[:, :type_count].reshape(-1, local_width)
    virtual_grads = jnp.einsum(
        "no,od->dn", virtual_key, w_key, preferred_element_type=jnp.float32
    ) + jnp.einsum("no,od->dn", virtual_value, w_value, preferred_element_type=jnp.float32)
    return (
        context.reshape(centres, head_count, length * HD),
        part_query,
        part_key,
        part_value,
        virtual_grads,
    )


def body(tokens, w_query, w_key, w_value, grad_out, owned_cls, send_rows, neigh_slot, neigh_count):
    centres = tokens.shape[0]
    model_width = tokens.shape[2]
    local_width = owned_cls.shape[0]
    own_rows = owned_cls.shape[1]
    type_count = neigh_slot.shape[1]
    slot_width = neigh_slot.shape[2]
    send_flat = send_rows[0].reshape(-1)
    outgoing = jnp.take(owned_cls, send_flat, axis=1)
    fetched = lax.all_to_all(outgoing, "nodes", split_axis=1, concat_axis=1, tiled=True)
    slots_total = fetched.shape[1]
    pairs = centres * type_count
    counts = neigh_count.reshape(-1).astype(jnp.float32)
    live_mask = lax.broadcasted_iota(jnp.int32, neigh_slot.shape, 2) < neigh_count[:, :, None]
    live_float = live_mask.astype(jnp.float32).reshape(-1)
    pair_index = lax.broadcasted_iota(jnp.int32, (pairs, slot_width), 0).reshape(-1)
    mixing = (
        jnp.zeros((pairs, slots_total), jnp.float32)
        .at[pair_index, neigh_slot.reshape(-1)]
        .add(live_float)
    )
    mixing_low = mixing.astype(jnp.bfloat16)
    full_table = widen_columns(fetched)
    summed = jnp.einsum("dr,nr->dn", full_table, mixing_low, preferred_element_type=jnp.float32)
    virtual_cols = (summed / counts[None, :]).astype(jnp.bfloat16)
    virtual = virtual_cols.T.reshape(centres, type_count, model_width)
    context, part_query, part_key, part_value, virtual_grads = local_attend(
        tokens, virtual, w_query, w_key, w_value, grad_out
    )
    summed_weights = lax.psum((part_query, part_key, part_value), "nodes")
    shared_grad = (
        lax.psum_scatter(
            virtual_grads.astype(jnp.bfloat16), "mp", scatter_dimension=0, tiled=True
        ).astype(jnp.float32)
        / counts[None, :]
    )
    slot_grads = jnp.dot(
        shared_grad, mixing, precision=lax.Precision.HIGHEST, preferred_element_type=jnp.float32
    )
    returned = lax.all_to_all(
        slot_grads.astype(jnp.bfloat16), "nodes", split_axis=1, concat_axis=1, tiled=True
    ).astype(slot_grads.dtype)
    grad_cls = jnp.zeros((local_width, own_rows), jnp.float32).at[:, send_flat].add(returned)
    return (context, summed_weights[0], summed_weights[1], summed_weights[2], grad_cls)


def solution(mesh):
    in_specs = (
        P("nodes", None, None),
        P("mp", None),
        P("mp", None),
        P("mp", None),
        P("nodes", "mp", None),
        P("mp", "nodes"),
        P("nodes", None, None),
        P("nodes", None, None),
        P("nodes", None),
    )
    out_specs = (
        P("nodes", "mp", None),
        P("mp", None),
        P("mp", None),
        P("mp", None),
        P("mp", "nodes"),
    )
    return jax.shard_map(body, mesh=mesh, in_specs=in_specs, out_specs=out_specs, check_vma=False)
```

profile of v0, /device:TPU:8, one launch (start us, length us, event | category | flops | bytes accessed | tf_op | source)
XLA Modules:
  0.0 523.2 jit_solution(8477868783395647791)
XLA Ops:
  10.4 7.5 %gather_fusion = bf16[2048,192]{1,0:T(8,128)(2,1)S(1)} fusion(bf16[192,2048]{0,1:T(8,128)(2,1)S(1)} %copy.75, s32[2048]{0:T(1024)S(1)} %broadcast_clamp_fusion), kind=kCustom, calls=%fused_computation | custom fusion | bytes 1581056 | tf_op jit(solution)/shard_map/jit(_take)/gather | solution.py:107
  18.5 40.3 %all_to_all.18 = bf16[192,64,32]{0,2,1:T(8,128)(2,1)} all-to-all(bf16[192,64,32]{0,2,1:T(8,128)(2,1)S(1)} %broadcast_select_fusion), channel_id=1, replica_groups=mesh['nodes'=64,'mp'=4] {'nodes'}, dimensions={1} | all-to-all | bytes 1572864 | tf_op jit(solution)/shard_map/all_to_all | solution.py:108
  61.7 12.3 %scatter_custom_fusion.1 = f32[131072]{0:T(1024)} fusion(s32[2048]{0:T(1024)S(1)} %broadcast_select_fusion.1, f32[2048]{0:T(1024)S(1)} %reshape.213, f32[]{:T(128)} %constant.8.clone.1), kind=kCustom, calls=%fused_computation.49 | custom fusion | flops 2048 | bytes 524292
  76.1 3.0 convolution_convert_fusion.2
  79.1 3.4 reshape.175
  82.6 3.5 reshape.183
  86.0 13.8 %all-gather.2.cloned.1.call-done = bf16[768,2048]{1,0:T(8,128)(2,1)} async-done(((bf16[192,2048]{1,0:T(8,128)(2,1)}), bf16[768,2048]{1,0:T(8,128)(2,1)}) %all-gather.2.cloned.1.call-update) | async-done | bytes 3145744 | tf_op jit(solution)/shard_map/all_gather | solution.py:11
  99.9 3.1 fusion.24
  103.7 4.6 pad_maximum_fusion
  108.3 3.1 reshape.179
  111.4 3.1 convolution_convert_fusion
  114.5 6.8 %reshape.181 = bf16[32,66,3,64]{1,0,3,2:T(8,128)(2,1)} reshape(bf16[2112,192]{0,1:T(8,128)(2,1)} %convolution_convert_fusion) | data formatting | bytes 1622016 | tf_op jit(solution)/shard_map/reshape | solution.py:36
  123.5 7.0 %reshape.180 = bf16[32,66,3,64]{1,0,3,2:T(8,128)(2,1)} reshape(bf16[2112,192]{0,1:T(8,128)(2,1)} %convolution_convert_fusion.1) | data formatting | bytes 1622016 | tf_op jit(solution)/shard_map/reshape | solution.py:31
  130.4 3.4 fusion.14
  133.9 3.2 fusion.49
  140.7 39.7 %fusion.10 = bf16[32,64,3,64]{1,3,2,0:T(8,128)(2,1)} fusion(f32[32,3,66,64]{2,3,1,0:T(8,128)} %fusion.18, bf16[32,66,3,64]{1,0,3,2:T(8,128)(2,1)} %reshape.180, f32[32,3,64,66]{3,2,1,0:T(8,128)} %get-tuple-element.29, f32[32,3,64]{2,1,0:T(4,128)} %get-tuple-element.28), kind=kOutput, calls=%fused_computation.26 | convolution fusion | flops 55142464 | bytes 4866048 | tf_op jit(solution)/shard_map/chlm,cmhe->clhe/dot_general | solution.py:61
  180.5 40.3 %fusion.11 = bf16[32,66,3,64]{1,3,2,0:T(8,128)(2,1)} fusion(f32[32,3,66,64]{2,3,1,0:T(8,128)} %fusion.18, bf16[32,64,3,64]{1,0,3,2:T(8,128)(2,1)} %reshape.175, f32[32,3,64,66]{3,2,1,0:T(8,128)} %get-tuple-element.29, f32[32,3,64]{2,1,0:T(4,128)} %get-tuple-element.28), kind=kOutput, calls=%fused_computation.27 | convolution fusion | flops 55154752 | bytes 4866048 | tf_op jit(solution)/shard_map/chlm,clhe->cmhe/dot_general | solution.py:64
  220.7 15.9 %fusion.12 = bf16[32,66,3,64]{1,3,2,0:T(8,128)(2,1)} fusion(bf16[32,3,64,64]{3,2,0,1:T(8,128)(2,1)} %reshape.183, f32[32,3,64]{2,1,0:T(4,128)} %get-tuple-element.28, f32[32,3,64,66]{3,2,1,0:T(8,128)} %copy-done.2), kind=kOutput, calls=%fused_computation.28 | convolution fusion | flops 54343744 | bytes 3244032 | tf_op jit(solution)/shard_map/chlm,chle->cmhe/dot_general | solution.py:52
  236.6 3.6 copy.85
  240.2 3.5 reshape.184
  243.7 3.6 copy.87
  247.3 4.2 reshape.185
  251.4 3.6 copy.89
  255.0 4.2 reshape.186
  275.8 19.8 %reduce-scatter.4.cloned.1.call-done = bf16[192,64]{1,0:T(8,128)(2,1)} async-done(((bf16[768,64]{1,0:T(8,128)(2,1)}), bf16[192,64]{1,0:T(8,128)(2,1)}) %reduce-scatter.4.cloned.1.call-update) | async-done | bytes 24592
  297.0 3.4 convolution_convert_fusion.3
  302.7 10.7 %all-to-all-start.1 = ((bf16[192,64,32]{0,2,1:T(8,128)(2,1)}), bf16[192,64,32]{0,2,1:T(8,128)(2,1)}, u32[]{:S(2)}, u32[]{:S(2)}) async-start(bf16[192,64,32]{0,2,1:T(8,128)(2,1)} %bitcast.91), calls=%async_computation.1 | async-start | bytes 2097152 | tf_op jit(solution)/shard_map/all_to_all | solution.py:138
  313.5 3.8 fusion.50
  319.0 14.1 %convolution_convert_fusion.7 = bf16[32,3,64,64]{3,2,1,0:T(8,128)(2,1)S(1)} fusion(bf16[32,66,3,64]{1,0,3,2:T(8,128)(2,1)} %reshape.181, f32[32,3,64]{2,1,0:T(4,128)} %get-tuple-element.28, f32[32,3,64,66]{3,2,1,0:T(8,128)} %copy-done.2), kind=kOutput, calls=%fused_computation.23 | convolution fusion | flops 54331456 | bytes 3244032 | tf_op jit(solution)/shard_map/chlm,cmhe->chle/dot_general | solution.py:45
  336.0 5.9 %all-to-all-done.1 = bf16[192,64,32]{0,2,1:T(8,128)(2,1)} async-done(((bf16[192,64,32]{0,2,1:T(8,128)(2,1)}), bf16[192,64,32]{0,2,1:T(8,128)(2,1)}, u32[]{:S(2)}, u32[]{:S(2)}) %all-to-all-start.1) | async-done | bytes 786464 | tf_op jit(solution)/shard_map/all_to_all | solution.py:138
  341.8 11.4 %scatter_custom_fusion = f32[192,2048]{0,1:T(8,128)S(1)} fusion(s32[2048]{0:T(1024)S(1)} %bitcast.95, bf16[192,2048]{0,1:T(8,128)(2,1)} %bitcast.16, f32[]{:T(128)} %constant.8.clone.1), kind=kCustom, calls=%fused_computation.19 | custom fusion | flops 786432 | bytes 2359300 | tf_op jit(solution)/shard_map/scatter-add | solution.py:141
  355.0 155.8 %all-reduce.3.cloned.1.call-done = (f32[192,768]{1,0:T(8,128)}, f32[192,768]{1,0:T(8,128)}, f32[192,768]{1,0:T(8,128)}) async-done(((f32[192,768]{1,0:T(8,128)}, f32[192,768]{1,0:T(8,128)}, f32[192,768]{1,0:T(8,128)}), (f32[192,768]{1,0:T(8,128)}, f32[192,768]{1,0:T(8,128)}, f32[192,768]{1,0:T(8,128)})) %all-reduce.3.cloned.1.call-update) | async-done | bytes 1769488 | tf_op jit(solution)/shard_map/psum | solution.py:128
  (69 shorter events, 47.5 us)
Async XLA Ops:
  7.2 114.2 %copy-start = (bf16[192,768]{1,0:T(8,128)(2,1)S(1)}, bf16[192,768]{1,0:T(8,128)(2,1)}, u32[]{:S(2)}) copy-start(bf16[192,768]{1,0:T(8,128)(2,1)} %param.11) | copy-start | bytes 884740
  7.2 92.7 %all-gather.2.cloned.1.call-start = ((), (), s32[]{:S(2)}) async-start(), calls=%async_computation.3 | async-start | bytes 3932160 | tf_op jit(solution)/shard_map/all_gather | solution.py:11
  17.9 43.0 %copy-start.7 = (s32[32,2]{0,1:T(2,128)S(1)}, s32[32,2]{0,1:T(2,128)}, u32[]{:S(2)}) copy-start(s32[32,2]{0,1:T(2,128)} %param.17) | copy-start | bytes 772
  18.0 43.1 %copy-start.6 = (s32[32,2,32]{2,1,0:T(2,128)S(1)}, s32[32,2,32]{2,1,0:T(2,128)}, u32[]{:S(2)}) copy-start(s32[32,2,32]{2,1,0:T(2,128)} %param.16) | copy-start | bytes 24580
  18.0 43.5 %copy-start.8 = (s32[2]{0:T(128)S(1)}, s32[2]{0:T(128)}, u32[]{:S(2)}) copy-start(s32[2]{0:T(128)} %constant.34) | copy-start | bytes 28
  18.0 43.6 %copy-start.9 = (s32[2]{0:T(128)S(1)}, s32[2]{0:T(128)}, u32[]{:S(2)}) copy-start(s32[2]{0:T(128)} %constant.37) | copy-start | bytes 28
  18.5 57.7 %copy-start.1 = (bf16[32,64,768]{2,1,0:T(8,128)(2,1)S(1)}, bf16[32,64,768]{2,1,0:T(8,128)(2,1)}, u32[]{:S(2)}) copy-start(bf16[32,64,768]{2,1,0:T(8,128)(2,1)} %param.9) | copy-start | bytes 9437188
  60.9 234.6 %reduce-scatter.4.cloned.1.call-start = ((), (), s32[]{:S(2)}) async-start(), calls=%async_computation.4 | async-start | bytes 245760
  133.9 3.3 copy-start.2
  133.9 3.3 copy-start.3
  133.9 4.2 copy-start.4
  302.7 39.1 %all-to-all-start.1 = ((bf16[192,64,32]{0,2,1:T(8,128)(2,1)}), bf16[192,64,32]{0,2,1:T(8,128)(2,1)}, u32[]{:S(2)}, u32[]{:S(2)}) async-start(bf16[192,64,32]{0,2,1:T(8,128)(2,1)} %bitcast.91), calls=%async_computation.1 | async-start | bytes 2097152 | tf_op jit(solution)/shard_map/all_to_all | solution.py:138
  313.4 197.3 %all-reduce.3.cloned.1.call-start = ((), (), s32[]{:S(2)}) async-start(), calls=%async_computation.5 | async-start | bytes 3538944 | tf_op jit(solution)/shard_map/psum | solution.py:128
  313.5 3.8 copy-start.5
Sparse Core Ops, SparseCore 0:
  61.0 38.7 all-gather.1
  273.1 22.4 reduce-scatter.3
  319.1 191.5 all-reduce.2
where the time goes:
time: 528 us; the launch traced here: 523 us
  waiting for transfers between devices  195 us (37%)
  matrix products  143 us (27%)
  local copies, waits for them, and re-layouts  86.9 us (16%)
  blocking collectives  40.3 us (8%)
  other arithmetic  33.1 us (6%)
  between operations  14.3 us (3%)
  starting transfers between devices  10.8 us (2%)
    psum x1, waiting for transfers between devices, body(): summed_weights = lax.psum((part_query, part_key, part_value), 'nodes')  156 us
    dot_general x1, matrix products, local_attend(): jnp.einsum('chlm,clhe->cmhe', score_low, queries, preferred_element_type=...  40.3 us
    all_to_all x1, blocking collectives, body(): lax.all_to_all(outgoing, 'nodes', split_axis=1, concat_axis=1, tiled=True)  40.3 us
    dot_general x1, matrix products, local_attend(): jnp.einsum('chlm,cmhe->clhe', score_low, keys, preferred_element_type=jnp...  39.7 us
    unnamed x4, waiting for transfers between devices  19.8 us
    dot_general x1, matrix products, local_attend(): jnp.einsum('chlm,chle->cmhe', probs_low, grad_heads, preferred_element_ty...  15.9 us
    dot_general x1, matrix products, local_attend(): jnp.einsum('chlm,cmhe->chle', probs_low, values, preferred_element_type=j...  14.1 us
    unnamed x29, local copies, waits for them, and re-layouts  14 us
  transfers between devices with their start and end apart: 4, of which 4 were waited for; matrix products, arithmetic and copies ran while one was open for 12% of the time, Pallas kernels for 0%

commit v1 on v0

--- a/solution.py
+++ b/solution.py
@@ -105,7 +105,10 @@
     slot_width = neigh_slot.shape[2]
     send_flat = send_rows[0].reshape(-1)
     outgoing = jnp.take(owned_cls, send_flat, axis=1)
-    fetched = lax.all_to_all(outgoing, "nodes", split_axis=1, concat_axis=1, tiled=True)
+    devices = lax.axis_size("nodes")
+    blocks = jnp.stack(jnp.split(outgoing, devices, axis=1), axis=0)
+    blocks = lax.all_to_all(blocks, "nodes", split_axis=0, concat_axis=0)
+    fetched = jnp.concatenate(blocks, axis=1)
     slots_total = fetched.shape[1]
     pairs = centres * type_count
     counts = neigh_count.reshape(-1).astype(jnp.float32)

time: 528 us -> 528 us (level)
    unnamed x29 -> x92, local copies, waits for them, and re-layouts: 14 us -> 14.2 us
where the time goes in v1:
time: 528 us; the launch traced here: 523 us
  waiting for transfers between devices  195 us (37%)
  matrix products  143 us (27%)
  local copies, waits for them, and re-layouts  87.1 us (16%)
  blocking collectives  40.3 us (8%)
  other arithmetic  32.4 us (6%)
  between operations  14.8 us (3%)
  starting transfers between devices  10.8 us (2%)
    psum x1, waiting for transfers between devices, body(): summed_weights = lax.psum((part_query, part_key, part_value), 'nodes')  156 us
    dot_general x1, matrix products, local_attend(): jnp.einsum('chlm,clhe->cmhe', score_low, queries, preferred_element_type=...  40.3 us
    all_to_all x1, blocking collectives, body(): blocks = lax.all_to_all(blocks, 'nodes', split_axis=0, concat_axis=0)  40.3 us
    dot_general x1, matrix products, local_attend(): jnp.einsum('chlm,cmhe->clhe', score_low, keys, preferred_element_type=jnp...  39.7 us
    unnamed x4, waiting for transfers between devices  19.8 us
    dot_general x1, matrix products, local_attend(): jnp.einsum('chlm,chle->cmhe', probs_low, grad_heads, preferred_element_ty...  15.9 us
    unnamed x92, local copies, waits for them, and re-layouts  14.2 us
    dot_general x1, matrix products, local_attend(): jnp.einsum('chlm,cmhe->chle', probs_low, values, preferred_element_type=j...  14.1 us
  transfers between devices with their start and end apart: 4, of which 4 were waited for; matrix products, arithmetic and copies ran while one was open for 12% of the time, Pallas kernels for 0%

profile of v1, /device:TPU:8, one launch (start us, length us, event | category | flops | bytes accessed | tf_op | source)
XLA Modules:
  0.0 523.2 jit_solution(7966686166117408120)
XLA Ops:
  9.7 7.5 %gather_fusion = bf16[2048,192]{1,0:T(8,128)(2,1)S(1)} fusion(bf16[192,2048]{0,1:T(8,128)(2,1)S(1)} %copy.52, s32[2048]{0:T(1024)S(1)} %broadcast_clamp_fusion), kind=kCustom, calls=%fused_computation | custom fusion | bytes 1581056 | tf_op jit(solution)/shard_map/jit(_take)/gather | solution.py:107
  18.5 40.3 %all_to_all.14 = bf16[64,192,32]{1,2,0:T(8,128)(2,1)} all-to-all(bf16[64,192,32]{1,2,0:T(8,128)(2,1)S(1)} %constant_dynamic-update-slice_fusion), channel_id=1, replica_groups=mesh['nodes'=64,'mp'=4] {'nodes'}, dimensions={0} | all-to-all | bytes 1572864 | tf_op jit(solution)/shard_map/all_to_all | solution.py:110
  61.7 12.3 %scatter_custom_fusion.1 = f32[131072]{0:T(1024)} fusion(s32[2048]{0:T(1024)S(1)} %broadcast_select_fusion, f32[2048]{0:T(1024)S(1)} %reshape.213, f32[]{:T(128)} %constant.8.clone.1), kind=kCustom, calls=%fused_computation.49 | custom fusion | flops 2048 | bytes 524292
  76.1 3.0 convolution_convert_fusion.2
  79.1 3.4 reshape.173
  82.6 3.5 reshape.183
  86.0 13.8 %all-gather.2.cloned.1.call-done = bf16[768,2048]{1,0:T(8,128)(2,1)} async-done(((bf16[192,2048]{1,0:T(8,128)(2,1)}), bf16[768,2048]{1,0:T(8,128)(2,1)}) %all-gather.2.cloned.1.call-update) | async-done | bytes 3145744 | tf_op jit(solution)/shard_map/all_gather | solution.py:11
  99.9 3.1 fusion.24
  103.7 4.6 pad_maximum_fusion
  108.3 3.1 reshape.179
  111.4 3.1 convolution_convert_fusion
  114.5 6.8 %reshape.181 = bf16[32,66,3,64]{1,0,3,2:T(8,128)(2,1)} reshape(bf16[2112,192]{0,1:T(8,128)(2,1)} %convolution_convert_fusion) | data formatting | bytes 1622016 | tf_op jit(solution)/shard_map/reshape | solution.py:36
  123.5 7.0 %reshape.180 = bf16[32,66,3,64]{1,0,3,2:T(8,128)(2,1)} reshape(bf16[2112,192]{0,1:T(8,128)(2,1)} %convolution_convert_fusion.1) | data formatting | bytes 1622016 | tf_op jit(solution)/shard_map/reshape | solution.py:31
  130.4 3.4 fusion.14
  133.9 3.2 fusion.49
  140.7 39.7 %fusion.10 = bf16[32,64,3,64]{1,3,2,0:T(8,128)(2,1)} fusion(f32[32,3,66,64]{2,3,1,0:T(8,128)} %fusion.18, bf16[32,66,3,64]{1,0,3,2:T(8,128)(2,1)} %reshape.180, f32[32,3,64,66]{3,2,1,0:T(8,128)} %get-tuple-element.24, f32[32,3,64]{2,1,0:T(4,128)} %get-tuple-element.23), kind=kOutput, calls=%fused_computation.26 | convolution fusion | flops 55142464 | bytes 4866048 | tf_op jit(solution)/shard_map/chlm,cmhe->clhe/dot_general | solution.py:61
  180.5 40.3 %fusion.11 = bf16[32,66,3,64]{1,3,2,0:T(8,128)(2,1)} fusion(f32[32,3,66,64]{2,3,1,0:T(8,128)} %fusion.18, bf16[32,64,3,64]{1,0,3,2:T(8,128)(2,1)} %reshape.173, f32[32,3,64,66]{3,2,1,0:T(8,128)} %get-tuple-element.24, f32[32,3,64]{2,1,0:T(4,128)} %get-tuple-element.23), kind=kOutput, calls=%fused_computation.27 | convolution fusion | flops 55154752 | bytes 4866048 | tf_op jit(solution)/shard_map/chlm,clhe->cmhe/dot_general | solution.py:64
  220.7 15.9 %fusion.12 = bf16[32,66,3,64]{1,3,2,0:T(8,128)(2,1)} fusion(bf16[32,3,64,64]{3,2,0,1:T(8,128)(2,1)} %reshape.183, f32[32,3,64]{2,1,0:T(4,128)} %get-tuple-element.23, f32[32,3,64,66]{3,2,1,0:T(8,128)} %copy-done.2), kind=kOutput, calls=%fused_computation.28 | convolution fusion | flops 54343744 | bytes 3244032 | tf_op jit(solution)/shard_map/chlm,chle->cmhe/dot_general | solution.py:52
  236.6 3.6 copy.62
  240.2 3.5 reshape.184
  243.7 3.6 copy.64
  247.3 4.2 reshape.185
  251.4 3.6 copy.66
  255.0 4.2 reshape.186
  275.8 19.8 %reduce-scatter.4.cloned.1.call-done = bf16[192,64]{1,0:T(8,128)(2,1)} async-done(((bf16[768,64]{1,0:T(8,128)(2,1)}), bf16[192,64]{1,0:T(8,128)(2,1)}) %reduce-scatter.4.cloned.1.call-update) | async-done | bytes 24592
  297.1 3.4 convolution_convert_fusion.3
  302.7 10.7 %all-to-all-start.1 = ((bf16[192,64,32]{0,2,1:T(8,128)(2,1)}), bf16[192,64,32]{0,2,1:T(8,128)(2,1)}, u32[]{:S(2)}, u32[]{:S(2)}) async-start(bf16[192,64,32]{0,2,1:T(8,128)(2,1)} %bitcast.344), calls=%async_computation.1 | async-start | bytes 2097152 | tf_op jit(solution)/shard_map/all_to_all | solution.py:141
  313.5 3.8 fusion.50
  319.0 14.1 %convolution_convert_fusion.7 = bf16[32,3,64,64]{3,2,1,0:T(8,128)(2,1)S(1)} fusion(bf16[32,66,3,64]{1,0,3,2:T(8,128)(2,1)} %reshape.181, f32[32,3,64]{2,1,0:T(4,128)} %get-tuple-element.23, f32[32,3,64,66]{3,2,1,0:T(8,128)} %copy-done.2), kind=kOutput, calls=%fused_computation.23 | convolution fusion | flops 54331456 | bytes 3244032 | tf_op jit(solution)/shard_map/chlm,cmhe->chle/dot_general | solution.py:45
  336.0 5.9 %all-to-all-done.1 = bf16[192,64,32]{0,2,1:T(8,128)(2,1)} async-done(((bf16[192,64,32]{0,2,1:T(8,128)(2,1)}), bf16[192,64,32]{0,2,1:T(8,128)(2,1)}, u32[]{:S(2)}, u32[]{:S(2)}) %all-to-all-start.1) | async-done | bytes 786464 | tf_op jit(solution)/shard_map/all_to_all | solution.py:141
  341.8 11.4 %scatter_custom_fusion = f32[192,2048]{0,1:T(8,128)S(1)} fusion(s32[2048]{0:T(1024)S(1)} %bitcast.347, bf16[192,2048]{0,1:T(8,128)(2,1)} %bitcast.79, f32[]{:T(128)} %constant.8.clone.1), kind=kCustom, calls=%fused_computation.19 | custom fusion | flops 786432 | bytes 2359300 | tf_op jit(solution)/shard_map/scatter-add | solution.py:144
  355.0 155.7 %all-reduce.3.cloned.1.call-done = (f32[192,768]{1,0:T(8,128)}, f32[192,768]{1,0:T(8,128)}, f32[192,768]{1,0:T(8,128)}) async-done(((f32[192,768]{1,0:T(8,128)}, f32[192,768]{1,0:T(8,128)}, f32[192,768]{1,0:T(8,128)}), (f32[192,768]{1,0:T(8,128)}, f32[192,768]{1,0:T(8,128)}, f32[192,768]{1,0:T(8,128)})) %all-reduce.3.cloned.1.call-update) | async-done | bytes 1769488 | tf_op jit(solution)/shard_map/psum | solution.py:131
  (133 shorter events, 47.0 us)
Async XLA Ops:
  7.2 114.2 %copy-start = (bf16[192,768]{1,0:T(8,128)(2,1)S(1)}, bf16[192,768]{1,0:T(8,128)(2,1)}, u32[]{:S(2)}) copy-start(bf16[192,768]{1,0:T(8,128)(2,1)} %param.11) | copy-start | bytes 884740
  7.2 92.7 %all-gather.2.cloned.1.call-start = ((), (), s32[]{:S(2)}) async-start(), calls=%async_computation.3 | async-start | bytes 3932160 | tf_op jit(solution)/shard_map/all_gather | solution.py:11
  17.9 43.1 %copy-start.7 = (s32[32,2]{0,1:T(2,128)S(1)}, s32[32,2]{0,1:T(2,128)}, u32[]{:S(2)}) copy-start(s32[32,2]{0,1:T(2,128)} %param.17) | copy-start | bytes 772
  17.9 43.2 %copy-start.6 = (s32[32,2,32]{2,1,0:T(2,128)S(1)}, s32[32,2,32]{2,1,0:T(2,128)}, u32[]{:S(2)}) copy-start(s32[32,2,32]{2,1,0:T(2,128)} %param.16) | copy-start | bytes 24580
  18.0 43.5 %copy-start.8 = (s32[2]{0:T(128)S(1)}, s32[2]{0:T(128)}, u32[]{:S(2)}) copy-start(s32[2]{0:T(128)} %constant.34) | copy-start | bytes 28
  18.0 43.6 %copy-start.9 = (s32[2]{0:T(128)S(1)}, s32[2]{0:T(128)}, u32[]{:S(2)}) copy-start(s32[2]{0:T(128)} %constant.37) | copy-start | bytes 28
  18.5 57.7 %copy-start.1 = (bf16[32,64,768]{2,1,0:T(8,128)(2,1)S(1)}, bf16[32,64,768]{2,1,0:T(8,128)(2,1)}, u32[]{:S(2)}) copy-start(bf16[32,64,768]{2,1,0:T(8,128)(2,1)} %param.9) | copy-start | bytes 9437188
  60.9 234.6 %reduce-scatter.4.cloned.1.call-start = ((), (), s32[]{:S(2)}) async-start(), calls=%async_computation.4 | async-start | bytes 245760
  133.9 3.3 copy-start.2
  133.9 3.3 copy-start.3
  133.9 4.2 copy-start.4
  302.7 39.1 %all-to-all-start.1 = ((bf16[192,64,32]{0,2,1:T(8,128)(2,1)}), bf16[192,64,32]{0,2,1:T(8,128)(2,1)}, u32[]{:S(2)}, u32[]{:S(2)}) async-start(bf16[192,64,32]{0,2,1:T(8,128)(2,1)} %bitcast.344), calls=%async_computation.1 | async-start | bytes 2097152 | tf_op jit(solution)/shard_map/all_to_all | solution.py:141
  313.4 197.2 %all-reduce.3.cloned.1.call-start = ((), (), s32[]{:S(2)}) async-start(), calls=%async_computation.5 | async-start | bytes 3538944 | tf_op jit(solution)/shard_map/psum | solution.py:131
  313.5 3.8 copy-start.5
Sparse Core Ops, SparseCore 0:
  61.1 38.7 all-gather.1
  273.1 22.4 reduce-scatter.3
  319.1 191.4 all-reduce.2
